TPU v7x, 32 devices: a whole 2x2x4 slice. The times are simulated.
32 devices in a mesh: rows: 16 (over z, y, x), cols: 2 (over core).
Axes of the slice: x: 2, y: 2, z: 4, core: 2. Of those that a mesh axis runs over, the one named last changes fastest.
Arguments:
- parent_front: float32 [4096, 2048], P('rows', 'cols')
- right_sides: float32 [4096, 64], P('rows'), may hold values from -6 to 6
- child_values: float32 [1024, 1024], P('rows', 'cols'), may hold values from -6 to 6
- block_owner: int32 [256], P('rows'), may hold values from 0 to 15, as said below
- row_map: int32 [1024], P('rows'), may hold values from 0 to 255
- col_map: int32 [1024], P('cols'), may hold values from 0 to 1023, as said below
Outputs:
- updated: float32 [4096, 2048], P('rows', 'cols')
- side_coeffs: float32 [128, 64], replicated
- side_left: float32 [4096, 64], P('rows')
Inputs may be any that keep to these rules, and one draw needn't show every extreme that they name: `block_owner`: for every k, entries k * 16 to (k + 1) * 16 - 1 form a permutation of 0 to 15. `col_map`: each aligned run of 512 entries is strictly increasing, starts with 0 and ends with 1023.
All inputs are finite; a program needn't handle non-finite values.
Results may differ from a plain program's by a relative error of at most 0.0003.
Values sent between devices are 32-bit elements; how exact they have to be, the bound alone decides.
A program may use at most 64 MiB of HBM per device.

v0:
```python
import jax
import jax.numpy as jnp
from jax import lax
from jax.sharding import PartitionSpec as P

PANEL = 128
highest = lax.Precision.HIGHEST


def spread_2(value, axis, source):
    kept = jnp.where(lax.axis_index(axis) == source, value, 0).astype(value.dtype)
    return lax.psum(kept, axis)


def swapped(block, axis, stride):
    count = lax.axis_size(axis)
    route = []
    for low in range(count):
        high = low | 1 << stride
        if high != low and high < count:
            route += [(low, high), (high, low)]
    return lax.ppermute(block, axis, route)


def matmul(left, right):
    return jnp.dot(left, right, precision=highest, preferred_element_type=jnp.float32)


def lower_inverse(lower):
    order = lower.shape[0]
    if order <= 16:
        return jax.scipy.linalg.solve_triangular(
            lower, jnp.eye(order, dtype=jnp.float32), lower=True
        )
    half = order // 2
    first_inv = lower_inverse(lower[:half, :half])
    second_inv = lower_inverse(lower[half:, half:])
    corner = -matmul(second_inv, matmul(lower[half:, :half], first_inv))
    top = jnp.concatenate([first_inv, jnp.zeros((half, order - half), jnp.float32)], axis=1)
    bottom = jnp.concatenate([corner, second_inv], axis=1)
    return jnp.concatenate([top, bottom], axis=0)


def shards(parent_front, right_sides, child_values, block_owner, row_map, col_map):
    blocks_count = lax.axis_size("rows")
    rows_dev, cols_dev = parent_front.shape
    child_rows, child_cols = child_values.shape
    block_rows = child_rows // blocks_count
    grouped = child_values.reshape(blocks_count, block_rows, child_cols)
    targets = row_map.astype(jnp.float32).reshape(blocks_count, block_rows)
    ordered = jnp.zeros_like(grouped).at[block_owner].set(grouped)
    placed = jnp.zeros_like(targets).at[block_owner].set(targets)
    spread = (
        jnp.zeros((blocks_count, block_rows, cols_dev), jnp.float32).at[:, :, col_map].set(ordered)
    )
    arrived, landing = (
        lax.all_to_all(spread, "rows", split_axis=0, concat_axis=0, tiled=True),
        lax.all_to_all(placed, "rows", split_axis=0, concat_axis=0, tiled=True),
    )
    where_rows = landing.reshape(-1).astype(jnp.int32)
    assembled = parent_front.at[where_rows].add(arrived.reshape(-1, cols_dev))
    panel_rows = spread_2(assembled[:, :PANEL], "cols", 0)
    stacked = jnp.concatenate([assembled, right_sides], axis=1)
    products = matmul(panel_rows.T, stacked)
    gram_matrix = matmul(panel_rows.T, panel_rows)
    lower = jnp.linalg.cholesky(gram_matrix)
    inverse = lower_inverse(lower)
    reduced = matmul(inverse, products)
    upper = lower.T
    levels = blocks_count.bit_length() - 1
    for level in range(levels):
        packed = jnp.concatenate([upper, reduced], axis=1)
        partner = swapped(packed, "rows", level)
        other_upper = partner[:, :PANEL]
        other_reduced = partner[:, PANEL:]
        node_gram = matmul(upper.T, upper) + matmul(other_upper.T, other_upper)
        lower = jnp.linalg.cholesky(node_gram)
        inverse = lower_inverse(lower)
        joined = matmul(upper.T, reduced) + matmul(other_upper.T, other_reduced)
        reduced = matmul(inverse, joined)
        upper = lower.T
    coefs = matmul(inverse.T, reduced)
    remainder = stacked - matmul(panel_rows, coefs)
    updated = remainder[:, :cols_dev]
    side_left = remainder[:, cols_dev:]
    side_coeffs = coefs[:, cols_dev:]
    return (updated, side_coeffs, side_left)


def solution(mesh):
    in_specs = (
        P("rows", "cols"),
        P("rows", None),
        P("rows", "cols"),
        P("rows"),
        P("rows"),
        P("cols"),
    )
    out_specs = (P("rows", "cols"), P(), P("rows", None))
    return jax.shard_map(shards, mesh=mesh, in_specs=in_specs, out_specs=out_specs, check_vma=False)
```

profile of v0, /device:TPU:0, one launch (start us, length us, event | category | flops | bytes accessed | tf_op | source)
XLA Modules:
  0.0 306.1 jit_solution(11291508165823120388)
XLA Ops:
  9.2 8.3 %all-to-all-start = ((f32[16,1,4]{2,1,0:T(1,128)}), f32[16,1,4]{2,1,0:T(1,128)S(1)}, u32[]{:S(2)}, u32[]{:S(2)}) async-start(f32[16,1,4]{2,1,0:T(1,128)} %bitcast.92), calls=%async_computation | async-start | bytes 16384 | tf_op jit(solution)/shard_map/all_to_all | solution.py:58
  19.3 13.6 %scatter_fusion.1 = f32[16,4,1024]{0,1,2:T(4,128)S(1)} fusion(f32[16,4,1024]{0,1,2:T(4,128)S(1)} %broadcast_in_dim.24, s32[512]{0:T(512)S(1)} %compare_select_fusion, f32[512,16,4]{1,2,0:T(4,128)S(1)} %copy.47), kind=kCustom, calls=%fused_computation.2 | custom fusion | bytes 395264 | tf_op jit(solution)/shard_map/scatter | solution.py:54
  32.9 1.4 copy.48
  34.3 7.0 %all-to-all-start.1 = ((f32[16,4,1024]{2,1,0:T(4,128)}), f32[16,4,1024]{2,1,0:T(4,128)S(1)}, u32[]{:S(2)}, u32[]{:S(2)}) async-start(f32[16,4,1024]{2,1,0:T(4,128)} %copy.48), calls=%async_computation.1 | async-start | bytes 524288 | tf_op jit(solution)/shard_map/all_to_all | solution.py:57
  41.6 9.1 %all-to-all-done.1 = f32[16,4,1024]{2,1,0:T(4,128)S(1)} async-done(((f32[16,4,1024]{2,1,0:T(4,128)}), f32[16,4,1024]{2,1,0:T(4,128)S(1)}, u32[]{:S(2)}, u32[]{:S(2)}) %all-to-all-start.1) | async-done | bytes 262176 | tf_op jit(solution)/shard_map/all_to_all | solution.py:57
  50.8 2.0 scatter_fusion.2
  53.9 15.6 %all-reduce.37.cloned.1.call-done = f32[256,128]{1,0:T(8,128)} async-done(((f32[256,128]{1,0:T(8,128)}), f32[256,128]{1,0:T(8,128)}) %all-reduce.37.cloned.1.call-update) | async-done | bytes 131088 | tf_op jit(solution)/shard_map/psum | solution.py:12
  69.5 1.4 fusion.448
  71.1 11.7 %cholesky.89 = f32[128,128]{1,0:T(8,128)S(1)} custom-call(f32[128,128]{1,0:T(8,128)S(1)} %fusion.141), custom_call_target="Cholesky" | custom-call | tf_op jit(solution)/shard_map/jit(cholesky)/cholesky | solution.py:66
  84.2 1.2 custom-call.46
  85.9 1.2 custom-call.50
  87.6 1.2 custom-call.48
  89.2 1.2 custom-call.49
  91.8 1.2 custom-call.44
  93.3 1.2 custom-call.45
  95.2 1.2 custom-call.47
  97.2 1.2 custom-call.51
  101.1 1.8 collective-permute-start
  103.8 13.6 %collective-permute-done = f32[128,1216]{0,1:T(8,128)S(1)} collective-permute-done((f32[128,1216]{0,1:T(8,128)S(1)}, f32[128,1216]{0,1:T(8,128)S(1)}, u32[]{:S(2)}, u32[]{:S(2)}) %collective-permute-start) | collective-permute-done | bytes 622624 | tf_op jit(solution)/shard_map/ppermute | solution.py:22
  117.7 11.8 %cholesky.100 = f32[128,128]{1,0:T(8,128)S(1)} custom-call(f32[128,128]{1,0:T(8,128)S(1)} %fusion.140), custom_call_target="Cholesky" | custom-call | tf_op jit(solution)/shard_map/jit(cholesky)/cholesky | solution.py:77
  131.7 1.2 custom-call.54
  133.3 1.2 custom-call.58
  135.0 1.2 custom-call.56
  136.6 1.2 custom-call.57
  138.5 1.2 custom-call.52
  140.1 1.2 custom-call.53
  141.9 1.2 custom-call.55
  144.0 1.2 custom-call.59
  147.4 1.8 collective-permute-start.1
  150.1 12.7 %collective-permute-done.1 = f32[128,1216]{0,1:T(8,128)S(1)} collective-permute-done((f32[128,1216]{0,1:T(8,128)S(1)}, f32[128,1216]{0,1:T(8,128)S(1)}, u32[]{:S(2)}, u32[]{:S(2)}) %collective-permute-start.1) | collective-permute-done | bytes 622624 | tf_op jit(solution)/shard_map/ppermute | solution.py:22
  163.2 11.7 %cholesky.111 = f32[128,128]{1,0:T(8,128)S(1)} custom-call(f32[128,128]{1,0:T(8,128)S(1)} %fusion.139), custom_call_target="Cholesky" | custom-call | tf_op jit(solution)/shard_map/jit(cholesky)/cholesky | solution.py:77
  182.0 1.2 custom-call.65
  185.4 1.2 custom-call.61
  187.2 1.2 custom-call.63
  189.3 1.2 custom-call.67
  192.7 1.8 collective-permute-start.2
  195.4 11.9 %collective-permute-done.2 = f32[128,1216]{0,1:T(8,128)S(1)} collective-permute-done((f32[128,1216]{0,1:T(8,128)S(1)}, f32[128,1216]{0,1:T(8,128)S(1)}, u32[]{:S(2)}, u32[]{:S(2)}) %collective-permute-start.2) | collective-permute-done | bytes 622624 | tf_op jit(solution)/shard_map/ppermute | solution.py:22
  207.6 11.9 %cholesky.122 = f32[128,128]{1,0:T(8,128)S(1)} custom-call(f32[128,128]{1,0:T(8,128)S(1)} %fusion.138), custom_call_target="Cholesky" | custom-call | tf_op jit(solution)/shard_map/jit(cholesky)/cholesky | solution.py:77
  226.6 1.2 custom-call.73
  230.1 1.2 custom-call.69
  231.9 1.2 custom-call.71
  237.3 2.7 collective-permute-start.3
  240.9 24.4 %collective-permute-done.3 = f32[128,1216]{0,1:T(8,128)S(1)} collective-permute-done((f32[128,1216]{0,1:T(8,128)S(1)}, f32[128,1216]{0,1:T(8,128)S(1)}, u32[]{:S(2)}, u32[]{:S(2)}) %collective-permute-start.3) | collective-permute-done | bytes 622624 | tf_op jit(solution)/shard_map/ppermute | solution.py:22
  265.7 11.7 %cholesky.133 = f32[128,128]{1,0:T(8,128)S(1)} custom-call(f32[128,128]{1,0:T(8,128)S(1)} %fusion.137), custom_call_target="Cholesky" | custom-call | tf_op jit(solution)/shard_map/jit(cholesky)/cholesky | solution.py:77
  283.8 1.2 custom-call.81
  287.2 1.4 custom-call.77
  289.2 1.2 custom-call.79
  297.7 1.3 copy.63
  (252 shorter events, 69.2 us)
Async XLA Ops:
  7.2 10.4 %copy-start.3 = (f32[64,512]{1,0:T(8,128)S(1)}, f32[64,512]{1,0:T(8,128)}, u32[]{:S(2)}) copy-start(f32[64,512]{1,0:T(8,128)} %param.11) | copy-start | bytes 393220
  7.2 0.7 copy-start.5
  7.2 0.7 copy-start.6
  7.2 10.3 %copy-start.4 = (s32[512]{0:T(512)S(1)}, s32[512]{0:T(512)}, u32[]{:S(2)}) copy-start(s32[512]{0:T(512)} %param.14) | copy-start | bytes 6148
  9.2 25.2 %all-to-all-start = ((f32[16,1,4]{2,1,0:T(1,128)}), f32[16,1,4]{2,1,0:T(1,128)S(1)}, u32[]{:S(2)}, u32[]{:S(2)}) async-start(f32[16,1,4]{2,1,0:T(1,128)} %bitcast.92), calls=%async_computation | async-start | bytes 16384 | tf_op jit(solution)/shard_map/all_to_all | solution.py:58
  34.3 16.5 %copy-start = (f32[256,1024]{1,0:T(8,128)S(1)}, f32[256,1024]{1,0:T(8,128)}, u32[]{:S(2)}) copy-start(f32[256,1024]{1,0:T(8,128)} %param.9) | copy-start | bytes 3145732
  34.3 16.4 %all-to-all-start.1 = ((f32[16,4,1024]{2,1,0:T(4,128)}), f32[16,4,1024]{2,1,0:T(4,128)S(1)}, u32[]{:S(2)}, u32[]{:S(2)}) async-start(f32[16,4,1024]{2,1,0:T(4,128)} %copy.48), calls=%async_computation.1 | async-start | bytes 524288 | tf_op jit(solution)/shard_map/all_to_all | solution.py:57
  41.4 28.1 %all-reduce.37.cloned.1.call-start = ((), (), s32[]{:S(2)}) async-start(), calls=%async_computation.2 | async-start | bytes 262144 | tf_op jit(solution)/shard_map/psum | solution.py:12
  53.9 45.4 %copy-start.2 = (f32[256,64]{0,1:T(8,128)S(1)}, f32[256,64]{0,1:T(8,128)}, u32[]{:S(2)}) copy-start(f32[256,64]{0,1:T(8,128)} %param.10) | copy-start | bytes 196612
  69.5 29.7 %copy-start.1 = (f32[256,128]{1,0:T(8,128)S(1)}, f32[256,128]{1,0:T(8,128)}, u32[]{:S(2)}) copy-start(f32[256,128]{1,0:T(8,128)} %all-reduce.37.cloned.1.call-done) | copy-start | bytes 393220
  101.1 16.3 %collective-permute-start = (f32[128,1216]{0,1:T(8,128)S(1)}, f32[128,1216]{0,1:T(8,128)S(1)}, u32[]{:S(2)}, u32[]{:S(2)}) collective-permute-start(f32[128,1216]{0,1:T(8,128)S(1)} %pad_maximum_fusion.2), channel_id=1, source_target_pairs={{0,2},{2,0},{4,6},{6,4},{8,10},{10,8},{12,14},{14,12},{16,18},{18,... | collective-permute-start | bytes 1867784 | tf_op jit(solution)/shard_map/ppermute | solution.py:22
  147.4 15.4 %collective-permute-start.1 = (f32[128,1216]{0,1:T(8,128)S(1)}, f32[128,1216]{0,1:T(8,128)S(1)}, u32[]{:S(2)}, u32[]{:S(2)}) collective-permute-start(f32[128,1216]{0,1:T(8,128)S(1)} %pad_maximum_fusion.3), channel_id=1, source_target_pairs={{0,4},{4,0},{2,6},{6,2},{8,12},{12,8},{10,14},{14,10},{16,20},{20,... | collective-permute-start | bytes 1867784 | tf_op jit(solution)/shard_map/ppermute | solution.py:22
  192.7 14.6 %collective-permute-start.2 = (f32[128,1216]{0,1:T(8,128)S(1)}, f32[128,1216]{0,1:T(8,128)S(1)}, u32[]{:S(2)}, u32[]{:S(2)}) collective-permute-start(f32[128,1216]{0,1:T(8,128)S(1)} %pad_maximum_fusion.4), channel_id=1, source_target_pairs={{0,8},{8,0},{2,10},{10,2},{4,12},{12,4},{6,14},{14,6},{16,24},{24,... | collective-permute-start | bytes 1867784 | tf_op jit(solution)/shard_map/ppermute | solution.py:22
  237.3 27.9 %collective-permute-start.3 = (f32[128,1216]{0,1:T(8,128)S(1)}, f32[128,1216]{0,1:T(8,128)S(1)}, u32[]{:S(2)}, u32[]{:S(2)}) collective-permute-start(f32[128,1216]{0,1:T(8,128)S(1)} %pad_maximum_fusion.5), channel_id=1, source_target_pairs={{0,16},{16,0},{2,18},{18,2},{4,20},{20,4},{6,22},{22,6},{8,24},{24... | collective-permute-start | bytes 1867784 | tf_op jit(solution)/shard_map/ppermute | solution.py:22
Sparse Core Ops, SparseCore 0:
  53.7 15.8 all-reduce.36
where the time goes:
time: 309 us; the launch traced here: 306 us
  other arithmetic  122 us (39%)
  waiting for transfers between devices  87.3 us (28%)
  matrix products  35.3 us (11%)
  starting transfers between devices  23.6 us (8%)
  local copies, waits for them, and re-layouts  22.5 us (7%)
  between operations  15.2 us (5%)
    ppermute x4, waiting for transfers between devices, swapped(): return lax.ppermute(block, axis, route)  62.6 us
    another operation x12, other arithmetic, shards(): lower = jnp.linalg.cholesky(node_gram)  49.9 us
    another operation x45, other arithmetic, lower_inverse(): jax.scipy.linalg.solve_triangular(lower, jnp.eye(order, dtype=jnp.float32...  49.9 us
    dot_general x95, matrix products, matmul(): jnp.dot(left, right, precision=highest, preferred_element_type=jnp.float32)  27.1 us
    psum x1, waiting for transfers between devices, spread_2(): return lax.psum(kept, axis)  15.6 us
    scatter x2, local copies, waits for them, and re-layouts, shards(): jnp.zeros((blocks_count, block_rows, cols_dev), jnp.float32)  15 us
    another operation x3, other arithmetic, shards(): lower = jnp.linalg.cholesky(gram_matrix)  12.4 us
    all_to_all x1, waiting for transfers between devices, shards(): lax.all_to_all(spread, 'rows', split_axis=0, concat_axis=0, tiled=True)  9.12 us
  transfers between devices with their start and end apart: 7, of which 6 were waited for; matrix products, arithmetic and copies ran while one was open for 7% of the time, Pallas kernels for 0%

commit v1 on v0

--- a/solution.py
+++ b/solution.py
@@ -9,7 +9,7 @@
 
 def spread_2(value, axis, source):
     kept = jnp.where(lax.axis_index(axis) == source, value, 0).astype(value.dtype)
-    return lax.psum(kept, axis)
+    return jnp.sum(lax.all_gather(kept, axis), axis=0)
 
 
 def swapped(block, axis, stride):

time: 309 us -> 280 us (0.906)
  between operations: 15.2 us -> 1.8 us
  waiting for transfers between devices: 87.3 us -> 75.6 us
  starting transfers between devices: 23.6 us -> 19.1 us
    psum x1 -> x0, waiting for transfers between devices: 15.6 us -> none  [spread_2(): return lax.psum(kept, axis)]
    ppermute x4, starting transfers between devices: 8.14 us -> 3.71 us  [swapped(): return lax.ppermute(block, axis, route)]
    ppermute x4, waiting for transfers between devices: 62.6 us -> 66.4 us  [swapped(): return lax.ppermute(block, axis, route)]
  transfers between devices with their start and end apart: 7 -> 6, of which waited for: 6 -> 5; matrix products, arithmetic and copies ran while one was open for 7% -> 7% of each run, Pallas kernels for 0% -> 0%
where the time goes in v1:
time: 280 us; the launch traced here: 277 us
  other arithmetic  121 us (43%)
  waiting for transfers between devices  75.6 us (27%)
  matrix products  34.2 us (12%)
  local copies, waits for them, and re-layouts  22.5 us (8%)
  starting transfers between devices  19.1 us (7%)
    ppermute x4, waiting for transfers between devices, swapped(): return lax.ppermute(block, axis, route)  66.4 us
    another operation x45, other arithmetic, lower_inverse(): jax.scipy.linalg.solve_triangular(lower, jnp.eye(order, dtype=jnp.float32...  49.9 us
    another operation x12, other arithmetic, shards(): lower = jnp.linalg.cholesky(node_gram)  49.9 us
    dot_general x95, matrix products, matmul(): jnp.dot(left, right, precision=highest, preferred_element_type=jnp.float32)  26 us
    scatter x2, local copies, waits for them, and re-layouts, shards(): jnp.zeros((blocks_count, block_rows, cols_dev), jnp.float32)  15 us
    another operation x3, other arithmetic, shards(): lower = jnp.linalg.cholesky(gram_matrix)  12.4 us
    all_to_all x1, waiting for transfers between devices, shards(): lax.all_to_all(spread, 'rows', split_axis=0, concat_axis=0, tiled=True)  9.17 us
    all_to_all x1, starting transfers between devices, shards(): lax.all_to_all(placed, 'rows', split_axis=0, concat_axis=0, tiled=True)  8.34 us
  transfers between devices with their start and end apart: 6, of which 5 were waited for; matrix products, arithmetic and copies ran while one was open for 7% of the time, Pallas kernels for 0%

profile of v1, /device:TPU:0, one launch (start us, length us, event | category | flops | bytes accessed | tf_op | source)
XLA Modules:
  0.0 276.9 jit_solution(575269598754322110)
XLA Ops:
  2.6 8.3 %all-to-all-start = ((f32[16,1,4]{2,1,0:T(1,128)}), f32[16,1,4]{2,1,0:T(1,128)S(1)}, u32[]{:S(2)}, u32[]{:S(2)}) async-start(f32[16,1,4]{2,1,0:T(1,128)} %bitcast.93), calls=%async_computation | async-start | bytes 16384 | tf_op jit(solution)/shard_map/all_to_all | solution.py:58
  12.8 13.6 %scatter_fusion.1 = f32[16,4,1024]{0,1,2:T(4,128)S(1)} fusion(f32[16,4,1024]{0,1,2:T(4,128)S(1)} %broadcast_in_dim.24, s32[512]{0:T(512)S(1)} %compare_select_fusion, f32[512,16,4]{1,2,0:T(4,128)S(1)} %copy.47), kind=kCustom, calls=%fused_computation.2 | custom fusion | bytes 395264 | tf_op jit(solution)/shard_map/scatter | solution.py:54
  26.4 1.4 copy.48
  27.8 7.0 %all-to-all-start.1 = ((f32[16,4,1024]{2,1,0:T(4,128)}), f32[16,4,1024]{2,1,0:T(4,128)S(1)}, u32[]{:S(2)}, u32[]{:S(2)}) async-start(f32[16,4,1024]{2,1,0:T(4,128)} %copy.48), calls=%async_computation.1 | async-start | bytes 524288 | tf_op jit(solution)/shard_map/all_to_all | solution.py:57
  35.0 9.2 %all-to-all-done.1 = f32[16,4,1024]{2,1,0:T(4,128)S(1)} async-done(((f32[16,4,1024]{2,1,0:T(4,128)}), f32[16,4,1024]{2,1,0:T(4,128)S(1)}, u32[]{:S(2)}, u32[]{:S(2)}) %all-to-all-start.1) | async-done | bytes 262176 | tf_op jit(solution)/shard_map/all_to_all | solution.py:57
  44.3 1.5 scatter_fusion.2
  45.8 2.5 all-gather
  48.9 11.7 %cholesky.89 = f32[128,128]{1,0:T(8,128)S(1)} custom-call(f32[128,128]{1,0:T(8,128)S(1)} %fusion.141), custom_call_target="Cholesky" | custom-call | tf_op jit(solution)/shard_map/jit(cholesky)/cholesky | solution.py:66
  62.0 1.2 custom-call.46
  63.7 1.2 custom-call.50
  65.3 1.2 custom-call.48
  67.0 1.2 custom-call.49
  69.9 1.2 custom-call.44
  71.5 1.2 custom-call.45
  73.3 1.2 custom-call.47
  75.3 1.2 custom-call.51
  80.9 14.4 %collective-permute-done = f32[128,1216]{0,1:T(8,128)S(1)} collective-permute-done((f32[128,1216]{0,1:T(8,128)S(1)}, f32[128,1216]{0,1:T(8,128)S(1)}, u32[]{:S(2)}, u32[]{:S(2)}) %collective-permute-start) | collective-permute-done | bytes 622624 | tf_op jit(solution)/shard_map/ppermute | solution.py:22
  95.7 11.9 %cholesky.100 = f32[128,128]{1,0:T(8,128)S(1)} custom-call(f32[128,128]{1,0:T(8,128)S(1)} %fusion.140), custom_call_target="Cholesky" | custom-call | tf_op jit(solution)/shard_map/jit(cholesky)/cholesky | solution.py:77
  109.6 1.2 custom-call.54
  111.3 1.2 custom-call.58
  113.0 1.2 custom-call.56
  114.6 1.2 custom-call.57
  116.5 1.2 custom-call.52
  118.1 1.2 custom-call.53
  119.9 1.2 custom-call.55
  122.0 1.2 custom-call.59
  127.2 13.4 %collective-permute-done.1 = f32[128,1216]{0,1:T(8,128)S(1)} collective-permute-done((f32[128,1216]{0,1:T(8,128)S(1)}, f32[128,1216]{0,1:T(8,128)S(1)}, u32[]{:S(2)}, u32[]{:S(2)}) %collective-permute-start.1) | collective-permute-done | bytes 622624 | tf_op jit(solution)/shard_map/ppermute | solution.py:22
  141.0 11.7 %cholesky.111 = f32[128,128]{1,0:T(8,128)S(1)} custom-call(f32[128,128]{1,0:T(8,128)S(1)} %fusion.139), custom_call_target="Cholesky" | custom-call | tf_op jit(solution)/shard_map/jit(cholesky)/cholesky | solution.py:77
  154.8 1.2 custom-call.62
  156.5 1.2 custom-call.66
  158.1 1.2 custom-call.64
  159.8 1.2 custom-call.65
  161.7 1.2 custom-call.60
  163.2 1.2 custom-call.61
  165.1 1.2 custom-call.63
  167.1 1.2 custom-call.67
  172.5 12.4 %collective-permute-done.2 = f32[128,1216]{0,1:T(8,128)S(1)} collective-permute-done((f32[128,1216]{0,1:T(8,128)S(1)}, f32[128,1216]{0,1:T(8,128)S(1)}, u32[]{:S(2)}, u32[]{:S(2)}) %collective-permute-start.2) | collective-permute-done | bytes 622624 | tf_op jit(solution)/shard_map/ppermute | solution.py:22
  185.3 11.9 %cholesky.122 = f32[128,128]{1,0:T(8,128)S(1)} custom-call(f32[128,128]{1,0:T(8,128)S(1)} %fusion.138), custom_call_target="Cholesky" | custom-call | tf_op jit(solution)/shard_map/jit(cholesky)/cholesky | solution.py:77
  199.3 1.2 custom-call.70
  204.3 1.2 custom-call.73
  207.8 1.2 custom-call.69
  209.6 1.2 custom-call.71
  216.6 26.2 %collective-permute-done.3 = f32[128,1216]{0,1:T(8,128)S(1)} collective-permute-done((f32[128,1216]{0,1:T(8,128)S(1)}, f32[128,1216]{0,1:T(8,128)S(1)}, u32[]{:S(2)}, u32[]{:S(2)}) %collective-permute-start.3) | collective-permute-done | bytes 622624 | tf_op jit(solution)/shard_map/ppermute | solution.py:22
  243.2 11.7 %cholesky.133 = f32[128,128]{1,0:T(8,128)S(1)} custom-call(f32[128,128]{1,0:T(8,128)S(1)} %fusion.137), custom_call_target="Cholesky" | custom-call | tf_op jit(solution)/shard_map/jit(cholesky)/cholesky | solution.py:77
  261.3 1.2 custom-call.81
  264.8 1.5 custom-call.77
  266.8 1.2 custom-call.79
  275.3 1.3 copy.63
  (249 shorter events, 66.4 us)
Async XLA Ops:
  0.6 10.4 %copy-start.2 = (f32[64,512]{1,0:T(8,128)S(1)}, f32[64,512]{1,0:T(8,128)}, u32[]{:S(2)}) copy-start(f32[64,512]{1,0:T(8,128)} %param.11) | copy-start | bytes 393220
  0.6 0.7 copy-start.4
  0.7 0.7 copy-start.5
  0.7 10.3 %copy-start.3 = (s32[512]{0:T(512)S(1)}, s32[512]{0:T(512)}, u32[]{:S(2)}) copy-start(s32[512]{0:T(512)} %param.14) | copy-start | bytes 6148
  2.6 25.2 %all-to-all-start = ((f32[16,1,4]{2,1,0:T(1,128)}), f32[16,1,4]{2,1,0:T(1,128)S(1)}, u32[]{:S(2)}, u32[]{:S(2)}) async-start(f32[16,1,4]{2,1,0:T(1,128)} %bitcast.93), calls=%async_computation | async-start | bytes 16384 | tf_op jit(solution)/shard_map/all_to_all | solution.py:58
  27.8 16.5 %copy-start = (f32[256,1024]{1,0:T(8,128)S(1)}, f32[256,1024]{1,0:T(8,128)}, u32[]{:S(2)}) copy-start(f32[256,1024]{1,0:T(8,128)} %param.9) | copy-start | bytes 3145732
  27.8 16.4 %all-to-all-start.1 = ((f32[16,4,1024]{2,1,0:T(4,128)}), f32[16,4,1024]{2,1,0:T(4,128)S(1)}, u32[]{:S(2)}, u32[]{:S(2)}) async-start(f32[16,4,1024]{2,1,0:T(4,128)} %copy.48), calls=%async_computation.1 | async-start | bytes 524288 | tf_op jit(solution)/shard_map/all_to_all | solution.py:57
  68.9 8.1 %copy-start.1 = (f32[256,64]{0,1:T(8,128)S(1)}, f32[256,64]{0,1:T(8,128)}, u32[]{:S(2)}) copy-start(f32[256,64]{0,1:T(8,128)} %param.10) | copy-start | bytes 196612
  79.2 16.1 %collective-permute-start = (f32[128,1216]{0,1:T(8,128)S(1)}, f32[128,1216]{0,1:T(8,128)S(1)}, u32[]{:S(2)}, u32[]{:S(2)}) collective-permute-start(f32[128,1216]{0,1:T(8,128)S(1)} %pad_maximum_fusion.2), channel_id=1, source_target_pairs={{0,2},{2,0},{4,6},{6,4},{8,10},{10,8},{12,14},{14,12},{16,18},{18,... | collective-permute-start | bytes 1867784 | tf_op jit(solution)/shard_map/ppermute | solution.py:22
  125.3 15.3 %collective-permute-start.1 = (f32[128,1216]{0,1:T(8,128)S(1)}, f32[128,1216]{0,1:T(8,128)S(1)}, u32[]{:S(2)}, u32[]{:S(2)}) collective-permute-start(f32[128,1216]{0,1:T(8,128)S(1)} %pad_maximum_fusion.3), channel_id=1, source_target_pairs={{0,4},{4,0},{2,6},{6,2},{8,12},{12,8},{10,14},{14,10},{16,20},{20,... | collective-permute-start | bytes 1867784 | tf_op jit(solution)/shard_map/ppermute | solution.py:22
  170.5 14.4 %collective-permute-start.2 = (f32[128,1216]{0,1:T(8,128)S(1)}, f32[128,1216]{0,1:T(8,128)S(1)}, u32[]{:S(2)}, u32[]{:S(2)}) collective-permute-start(f32[128,1216]{0,1:T(8,128)S(1)} %pad_maximum_fusion.4), channel_id=1, source_target_pairs={{0,8},{8,0},{2,10},{10,2},{4,12},{12,4},{6,14},{14,6},{16,24},{24,... | collective-permute-start | bytes 1867784 | tf_op jit(solution)/shard_map/ppermute | solution.py:22
  215.0 27.8 %collective-permute-start.3 = (f32[128,1216]{0,1:T(8,128)S(1)}, f32[128,1216]{0,1:T(8,128)S(1)}, u32[]{:S(2)}, u32[]{:S(2)}) collective-permute-start(f32[128,1216]{0,1:T(8,128)S(1)} %pad_maximum_fusion.5), channel_id=1, source_target_pairs={{0,16},{16,0},{2,18},{18,2},{4,20},{20,4},{6,22},{22,6},{8,24},{24... | collective-permute-start | bytes 1867784 | tf_op jit(solution)/shard_map/ppermute | solution.py:22
